TPU v7x, 768 devices: a whole 4x8x12 slice. The times are simulated.
768 devices in a mesh: xs: 16 (over y, z_hi), ys: 48 (over z_lo, x, core).
Axes of the slice: x: 4, y: 8, z: 12 (z_hi: 2, z_lo: 6; z = z_hi * 6 + z_lo), core: 2. Of those that a mesh axis runs over, the one named last changes fastest.
Arguments:
- fields: float32 [6, 16, 512, 6144], P(None, None, 'xs', 'ys'), may hold values from -6 to 6
- permittivity: float32 [16, 512, 6144], P(None, 'xs', 'ys'), may hold values from 1 to 12
- adj_values: float32 [73728, 128], P(('xs', 'ys')), may hold values from -6 to 6
- adj_owner: int32 [73728, 1], P(('xs', 'ys')), may hold values from 0 to 47; in each aligned block of 96 rows (0 to 95, 96 to 191, ...) at most 4 rows name the same one
- adj_row: int32 [73728], P(('xs', 'ys')), may hold values from 0 to 31
- angle_wave: int32 [128], replicated, may hold values from 0 to 4999
Outputs:
- new_fields: float32 [6, 16, 512, 6144], P(None, None, 'xs', 'ys')
- far_field: float32 [128, 2, 4, 6144], P('xs', None, None, 'ys')
Inputs may be any that keep to these rules, and one draw needn't show every extreme that they name: `adj_owner`: among the 96 rows of one device no ys index is named more than 4 times.
All inputs are finite; a program needn't handle non-finite values.
Results may differ from a plain program's by a relative error of at most 0.000071.
Values sent between devices are 32-bit elements; how exact they have to be, the bound alone decides.
A program may use at most 64 MiB of HBM per device.

v0:
```python
import math

import jax
import jax.numpy as jnp
from jax import lax
from jax.sharding import PartitionSpec as P

STEPS = 3
CAP = 4
GRID_X = 5000
X0 = 2000
ZS = 8


time_step = 0.5


def from_behind(block, axis, distance):
    devices = range(lax.axis_size(axis))
    route = [(i - distance, i) for i in devices if i - distance in devices]
    return lax.ppermute(block, axis, route)


def along_next(inner, edge, axis):
    return jnp.concatenate([lax.slice_in_dim(inner, 1, inner.shape[axis], axis=axis), edge], axis)


def along_prev(inner, edge, axis):
    return jnp.concatenate(
        [edge, lax.slice_in_dim(inner, 0, inner.shape[axis] - 1, axis=axis)], axis
    )


def across_x(plane, offset):
    return from_behind(plane, "xs", offset)


def across_y(plane, offset):
    return from_behind(plane, "ys", offset)


def from_next_x(plane):
    return across_x(plane, -1)


def from_next_y(plane):
    return across_y(plane, -1)


def from_prev_x(plane):
    return across_x(plane, 1)


def from_prev_y(plane):
    return across_y(plane, 1)


def advance(fields, coeffs, source, next_x, next_y, prev_x, prev_y):
    elec = [fields[0], fields[1], fields[2]]
    magn = [fields[3], fields[4], fields[5]]
    zero_layer = jnp.zeros((1,) + elec[0].shape[1:], jnp.float32)
    edge_x = next_x(jnp.stack([elec[1][:, 0, :], elec[2][:, 0, :]]))
    edge_y = next_y(jnp.stack([elec[0][:, :, 0], elec[2][:, :, 0]]))
    ey_xnext = along_next(elec[1], edge_x[0][:, None, :], 1)
    ez_xnext = along_next(elec[2], edge_x[1][:, None, :], 1)
    ex_ynext = along_next(elec[0], edge_y[0][:, :, None], 2)
    ez_ynext = along_next(elec[2], edge_y[1][:, :, None], 2)
    ex_znext = along_next(elec[0], zero_layer, 0)
    ey_znext = along_next(elec[1], zero_layer, 0)
    hx_new = magn[0] - time_step * (ez_ynext - elec[2] - (ey_znext - elec[1]))
    hy_new = magn[1] - time_step * (ex_znext - elec[0] - (ez_xnext - elec[2]))
    hz_new = magn[2] - time_step * (ey_xnext - elec[1] - (ex_ynext - elec[0]))
    back_x = prev_x(jnp.stack([hy_new[:, -1, :], hz_new[:, -1, :]]))
    back_y = prev_y(jnp.stack([hx_new[:, :, -1], hz_new[:, :, -1]]))
    hy_xprev = along_prev(hy_new, back_x[0][:, None, :], 1)
    hz_xprev = along_prev(hz_new, back_x[1][:, None, :], 1)
    hx_yprev = along_prev(hx_new, back_y[0][:, :, None], 2)
    hz_yprev = along_prev(hz_new, back_y[1][:, :, None], 2)
    hx_zprev = along_prev(hx_new, zero_layer, 0)
    hy_zprev = along_prev(hy_new, zero_layer, 0)
    ex_new = elec[0] + coeffs * (hz_new - hz_yprev - (hy_new - hy_zprev))
    ey_new = elec[1] + coeffs * (hx_new - hx_zprev - (hz_new - hz_xprev))
    ez_new = elec[2] + coeffs * (hy_new - hy_xprev - (hx_new - hx_yprev) - source)
    return jnp.stack([ex_new, ey_new, ez_new, hx_new, hy_new, hz_new])


def spectrum(tile, angles, first_x):
    positions = X0 + first_x + jnp.arange(tile.shape[1], dtype=jnp.int32)
    phase = angles[:, None] * positions[None, :] % GRID_X
    angle = phase.astype(jnp.float32) * (2.0 * math.pi / GRID_X)
    cosine = jnp.cos(angle)
    sine = -jnp.sin(angle)
    real_part = jnp.einsum("ax,cxy->acy", cosine, tile, precision=lax.Precision.HIGHEST)
    imag_part = jnp.einsum("ax,cxy->acy", sine, tile, precision=lax.Precision.HIGHEST)
    return jnp.stack([real_part, imag_part], axis=1)


def on_device(fields, permittivity, adj_values, adj_owner, adj_row, angle_wave):
    cells_x = fields.shape[2]
    cells_y = fields.shape[3]
    layers = fields.shape[1]
    groups = lax.axis_size("ys")
    total_x = cells_x * lax.axis_size("xs")
    per_block = angle_wave.shape[0] // lax.axis_size("xs")
    owners = adj_owner[:, 0]
    hits = (owners[:, None] == jnp.arange(groups, dtype=jnp.int32)[None, :]).astype(jnp.int32)
    before = jnp.cumsum(hits, axis=0) - hits
    slot_index = owners * CAP + jnp.sum(before * hits, axis=1)
    placing = (jnp.arange(groups * CAP, dtype=jnp.int32)[:, None] == slot_index[None, :]).astype(
        jnp.float32
    )
    outgoing = jnp.dot(placing, adj_values, precision=lax.Precision.HIGHEST).reshape(
        groups, CAP, cells_y
    )
    out_rows = jnp.dot(
        placing, adj_row.astype(jnp.float32), precision=lax.Precision.HIGHEST
    ).reshape(groups, CAP)
    incoming, in_rows = (
        lax.all_to_all(outgoing, "ys", split_axis=0, concat_axis=0, tiled=True),
        lax.all_to_all(out_rows, "ys", split_axis=0, concat_axis=0, tiled=True),
    )
    landing = (
        jnp.arange(cells_x, dtype=jnp.float32)[:, None] == in_rows.reshape(-1)[None, :]
    ).astype(jnp.float32)
    current = jnp.dot(
        landing, incoming.reshape(groups * CAP, cells_y), precision=lax.Precision.HIGHEST
    )
    coeffs = time_step / permittivity
    layer_mask = (jnp.arange(layers, dtype=jnp.int32) == ZS).astype(jnp.float32)[:, None, None]
    source = layer_mask * current[None]
    for iteration in range(STEPS):
        fields = advance(fields, coeffs, source, from_next_x, from_next_y, from_prev_x, from_prev_y)
    tile = jnp.stack([-fields[4][ZS], fields[3][ZS], fields[1][ZS], -fields[0][ZS]])
    my_angles = lax.dynamic_slice_in_dim(angle_wave, lax.axis_index("xs") * per_block, per_block)
    summed = spectrum(lax.all_gather(tile, "xs", axis=1, tiled=True), my_angles, jnp.int32(0))
    far_field = summed / math.sqrt(total_x)
    return (fields, far_field)


def solution(mesh):
    placed = (
        P(None, None, "xs", "ys"),
        P(None, "xs", "ys"),
        P(("xs", "ys"), None),
        P(("xs", "ys"), None),
        P(("xs", "ys")),
        P(),
    )
    return jax.shard_map(
        on_device,
        mesh=mesh,
        in_specs=placed,
        out_specs=(P(None, None, "xs", "ys"), P("xs", None, None, "ys")),
        check_vma=False,
    )
```

profile of v0, /device:TPU:2, one launch (start us, length us, event | category | flops | bytes accessed | tf_op | source)
XLA Modules:
  0.0 277.2 jit_solution(11644130007860939440)
XLA Ops:
  7.2 1.3 fusion.92
  8.7 1.9 collective-permute-start.1
  11.6 1.3 collective-permute-start
  13.4 0.8 all_to_all.9
  14.3 15.6 %all-to-all-start = ((f32[48,1,4]{2,1,0:T(1,128)}), f32[48,1,4]{2,1,0:T(1,128)S(1)}, u32[]{:S(2)}, u32[]{:S(2)}) async-start(f32[48,1,4]{2,1,0:T(1,128)} %bitcast.26), calls=%async_computation | async-start | bytes 49152 | tf_op jit(solution)/shard_map/all_to_all | solution.py:120
  29.8 0.7 slice_bitcast_fusion.2
  30.5 0.8 fusion.55
  31.9 0.8 slice.394
  32.8 0.7 slice.386
  33.8 5.5 %all-to-all-done = f32[48,1,4]{2,1,0:T(1,128)S(1)} async-done(((f32[48,1,4]{2,1,0:T(1,128)}), f32[48,1,4]{2,1,0:T(1,128)S(1)}, u32[]{:S(2)}, u32[]{:S(2)}) %all-to-all-start) | async-done | bytes 800 | tf_op jit(solution)/shard_map/all_to_all | solution.py:120
  39.3 5.5 %all-to-all-start.1 = ((f32[48,4,128]{2,1,0:T(4,128)}), f32[48,4,128]{2,1,0:T(4,128)S(1)}, u32[]{:S(2)}, u32[]{:S(2)}) async-start(f32[48,4,128]{2,1,0:T(4,128)} %bitcast.27), calls=%async_computation.1 | async-start | bytes 196608 | tf_op jit(solution)/shard_map/all_to_all | solution.py:119
  47.4 0.9 copy.207
  48.3 0.9 copy.204
  49.2 0.8 fusion.98
  50.0 1.4 fusion.12
  52.4 2.1 collective-permute-start.2
  55.9 11.3 %collective-permute-start.3 = (f32[2,16,128]{2,1,0:T(8,128)S(1)}, f32[2,16,128]{2,1,0:T(8,128)S(1)}, u32[]{:S(2)}, u32[]{:S(2)}) collective-permute-start(f32[2,16,128]{2,1,0:T(8,128)S(1)} %pad_maximum_fusion.4), channel_id=1, source_target_pairs={{0,48},{48,96},{96,144},{144,192},{192,240},{240,288},{288,336},{3... | collective-permute-start | bytes 49160 | tf_op jit(solution)/shard_map/ppermute | solution.py:21
  67.3 0.9 copy.212
  68.2 0.9 copy.218
  69.9 1.7 fusion.1
  72.0 3.2 %collective-permute-start.5 = (f32[2,16,32]{2,1,0:T(8,128)S(1)}, f32[2,16,32]{2,1,0:T(8,128)S(1)}, u32[]{:S(2)}, u32[]{:S(2)}) collective-permute-start(f32[2,16,32]{2,1,0:T(8,128)S(1)} %pad_maximum_fusion.6), channel_id=1, source_target_pairs={{1,0},{2,1},{3,2},{4,3},{5,4},{6,5},{7,6},{8,7},{9,8},{10,9},{11,1... | collective-permute-start | bytes 12296 | tf_op jit(solution)/shard_map/ppermute | solution.py:21
  75.5 0.7 slice.428
  77.7 1.3 collective-permute-start.4
  79.0 0.9 copy.221
  79.9 0.9 copy.222
  80.7 8.9 %collective-permute-done.4 = f32[2,16,128]{2,1,0:T(8,128)S(1)} collective-permute-done((f32[2,16,128]{2,1,0:T(8,128)S(1)}, f32[2,16,128]{2,1,0:T(8,128)S(1)}, u32[]{:S(2)}, u32[]{:S(2)}) %collective-permute-start.4) | collective-permute-done | bytes 16416 | tf_op jit(solution)/shard_map/ppermute | solution.py:21
  89.6 1.8 fusion.34
  91.9 1.9 collective-permute-start.6
  94.6 10.6 %collective-permute-start.7 = (f32[2,16,128]{2,1,0:T(8,128)S(1)}, f32[2,16,128]{2,1,0:T(8,128)S(1)}, u32[]{:S(2)}, u32[]{:S(2)}) collective-permute-start(f32[2,16,128]{2,1,0:T(8,128)S(1)} %pad_maximum_fusion.8), channel_id=1, source_target_pairs={{0,48},{48,96},{96,144},{144,192},{192,240},{240,288},{288,336},{3... | collective-permute-start | bytes 49160 | tf_op jit(solution)/shard_map/ppermute | solution.py:21
  105.6 1.0 collective-permute-done.7
  106.7 1.4 fusion.37
  108.5 2.8 %collective-permute-start.9 = (f32[2,16,32]{2,1,0:T(8,128)S(1)}, f32[2,16,32]{2,1,0:T(8,128)S(1)}, u32[]{:S(2)}, u32[]{:S(2)}) collective-permute-start(f32[2,16,32]{2,1,0:T(8,128)S(1)} %pad_maximum_fusion.10), channel_id=1, source_target_pairs={{1,0},{2,1},{3,2},{4,3},{5,4},{6,5},{7,6},{8,7},{9,8},{10,9},{11,1... | collective-permute-start | bytes 12296 | tf_op jit(solution)/shard_map/ppermute | solution.py:21
  111.6 0.7 slice.456
  113.7 1.3 collective-permute-start.8
  115.0 0.9 copy.231
  115.9 0.9 copy.232
  116.8 8.9 %collective-permute-done.8 = f32[2,16,128]{2,1,0:T(8,128)S(1)} collective-permute-done((f32[2,16,128]{2,1,0:T(8,128)S(1)}, f32[2,16,128]{2,1,0:T(8,128)S(1)}, u32[]{:S(2)}, u32[]{:S(2)}) %collective-permute-start.8) | collective-permute-done | bytes 16416 | tf_op jit(solution)/shard_map/ppermute | solution.py:21
  125.6 1.7 fusion.44
  127.9 1.9 collective-permute-start.10
  130.0 11.1 %collective-permute-start.11 = (f32[2,16,128]{2,1,0:T(8,128)S(1)}, f32[2,16,128]{2,1,0:T(8,128)S(1)}, u32[]{:S(2)}, u32[]{:S(2)}) collective-permute-start(f32[2,16,128]{2,1,0:T(8,128)S(1)} %pad_maximum_fusion.12), channel_id=1, source_target_pairs={{0,48},{48,96},{96,144},{144,192},{192,240},{240,288},{288,336},{3... | collective-permute-start | bytes 49160 | tf_op jit(solution)/shard_map/ppermute | solution.py:21
  141.5 1.0 collective-permute-done.11
  142.7 1.1 copy-done.8
  144.8 0.9 fusion.7
  145.7 0.7 bitcast_dynamic-update-slice_fusion.2
  146.4 0.7 bitcast_dynamic-update-slice_fusion.1
  147.1 0.7 bitcast_dynamic-update-slice_fusion
  147.8 119.1 %all-gather.2.cloned.1.call-done = f32[4,512,128]{2,1,0:T(8,128)} async-done(((f32[4,32,128]{2,1,0:T(8,128)}), f32[4,512,128]{2,1,0:T(8,128)}) %all-gather.2.cloned.1.call-update) | async-done | bytes 1048592 | tf_op jit(solution)/shard_map/all_gather | solution.py:135
  267.0 2.0 convolution_bitcast_fusion.1
  (132 shorter events, 17.3 us)
Async XLA Ops:
  7.2 23.4 %copy-start = (f32[96,128]{1,0:T(8,128)S(1)}, f32[96,128]{1,0:T(8,128)}, u32[]{:S(2)}) copy-start(f32[96,128]{1,0:T(8,128)} %param.8) | copy-start | bytes 147460
  7.2 22.6 %copy-start.1 = (f32[6,16,32,128]{3,2,1,0:T(8,128)S(1)}, f32[6,16,32,128]{3,2,1,0:T(8,128)}, u32[]{:S(2)}) copy-start(f32[6,16,32,128]{3,2,1,0:T(8,128)} %param.6) | copy-start | bytes 4718596
  7.2 5.7 %copy-start.11 = (s32[96,1]{0,1:T(1,128)S(1)}, s32[96,1]{0,1:T(1,128)}, u32[]{:S(2)}) copy-start(s32[96,1]{0,1:T(1,128)} %param.9) | copy-start | bytes 1156
  7.2 6.1 %copy-start.12 = (s32[96]{0:T(128)S(1)}, s32[96]{0:T(128)}, u32[]{:S(2)}) copy-start(s32[96]{0:T(128)} %param.10) | copy-start | bytes 1156
  8.7 38.1 %collective-permute-start.1 = (f32[2,16,32]{2,1,0:T(8,128)S(1)}, f32[2,16,32]{2,1,0:T(8,128)S(1)}, u32[]{:S(2)}, u32[]{:S(2)}) collective-permute-start(f32[2,16,32]{2,1,0:T(8,128)S(1)} %pad_maximum_fusion.2), channel_id=1, source_target_pairs={{1,0},{2,1},{3,2},{4,3},{5,4},{6,5},{7,6},{8,7},{9,8},{10,9},{11,1... | collective-permute-start | bytes 12296 | tf_op jit(solution)/shard_map/ppermute | solution.py:21
  11.6 37.6 %collective-permute-start = (f32[2,16,128]{2,1,0:T(8,128)}, f32[2,16,128]{2,1,0:T(8,128)}, u32[]{:S(2)}, u32[]{:S(2)}) collective-permute-start(f32[2,16,128]{2,1,0:T(8,128)} %pad_maximum_fusion.1), channel_id=1, source_target_pairs={{48,0},{96,48},{144,96},{192,144},{240,192},{288,240},{336,288},{3... | collective-permute-start | bytes 49160 | tf_op jit(solution)/shard_map/ppermute | solution.py:21
  14.3 25.1 %all-to-all-start = ((f32[48,1,4]{2,1,0:T(1,128)}), f32[48,1,4]{2,1,0:T(1,128)S(1)}, u32[]{:S(2)}, u32[]{:S(2)}) async-start(f32[48,1,4]{2,1,0:T(1,128)} %bitcast.26), calls=%async_computation | async-start | bytes 49152 | tf_op jit(solution)/shard_map/all_to_all | solution.py:120
  32.8 17.2 %copy-start.4 = (f32[16,32,127]{2,0,1:T(8,128)S(1)}, f32[16,32,127]{2,0,1:T(8,128)}, u32[]{:S(2)}) copy-start(f32[16,32,127]{2,0,1:T(8,128)} %slice.394) | copy-start | bytes 780292
  39.3 30.4 %all-to-all-start.1 = ((f32[48,4,128]{2,1,0:T(4,128)}), f32[48,4,128]{2,1,0:T(4,128)S(1)}, u32[]{:S(2)}, u32[]{:S(2)}) async-start(f32[48,4,128]{2,1,0:T(4,128)} %bitcast.27), calls=%async_computation.1 | async-start | bytes 196608 | tf_op jit(solution)/shard_map/all_to_all | solution.py:119
  44.9 222.1 %all-gather.2.cloned.1.call-start = ((), (), s32[]{:S(2)}) async-start(), calls=%async_computation.2 | async-start | bytes 1114112 | tf_op jit(solution)/shard_map/all_gather | solution.py:135
  49.2 2.2 copy-start.5
  51.8 17.9 %copy-start.10 = (f32[192]{0:T(256)S(1)}, f32[192]{0:T(256)}, u32[]{:S(2)}) copy-start(f32[192]{0:T(256)} %eq.58) | copy-start | bytes 2308
  51.9 18.0 %copy-start.2 = (f32[16,32,128]{2,1,0:T(8,128)S(1)}, f32[16,32,128]{2,1,0:T(8,128)}, u32[]{:S(2)}) copy-start(f32[16,32,128]{2,1,0:T(8,128)} %param.7) | copy-start | bytes 786436
  52.4 14.9 %collective-permute-start.2 = (f32[2,16,32]{2,1,0:T(8,128)S(1)}, f32[2,16,32]{2,1,0:T(8,128)S(1)}, u32[]{:S(2)}, u32[]{:S(2)}) collective-permute-start(f32[2,16,32]{2,1,0:T(8,128)S(1)} %pad_maximum_fusion.3), channel_id=1, source_target_pairs={{0,1},{1,2},{2,3},{3,4},{4,5},{5,6},{6,7},{7,8},{8,9},{9,10},{10,1... | collective-permute-start | bytes 12296 | tf_op jit(solution)/shard_map/ppermute | solution.py:21
  55.9 13.1 %collective-permute-start.3 = (f32[2,16,128]{2,1,0:T(8,128)S(1)}, f32[2,16,128]{2,1,0:T(8,128)S(1)}, u32[]{:S(2)}, u32[]{:S(2)}) collective-permute-start(f32[2,16,128]{2,1,0:T(8,128)S(1)} %pad_maximum_fusion.4), channel_id=1, source_target_pairs={{0,48},{48,96},{96,144},{144,192},{192,240},{240,288},{288,336},{3... | collective-permute-start | bytes 49160 | tf_op jit(solution)/shard_map/ppermute | solution.py:21
  69.9 1.7 copy-start.6
  72.0 7.0 %collective-permute-start.5 = (f32[2,16,32]{2,1,0:T(8,128)S(1)}, f32[2,16,32]{2,1,0:T(8,128)S(1)}, u32[]{:S(2)}, u32[]{:S(2)}) collective-permute-start(f32[2,16,32]{2,1,0:T(8,128)S(1)} %pad_maximum_fusion.6), channel_id=1, source_target_pairs={{1,0},{2,1},{3,2},{4,3},{5,4},{6,5},{7,6},{8,7},{9,8},{10,9},{11,1... | collective-permute-start | bytes 12296 | tf_op jit(solution)/shard_map/ppermute | solution.py:21
  77.7 11.9 %collective-permute-start.4 = (f32[2,16,128]{2,1,0:T(8,128)S(1)}, f32[2,16,128]{2,1,0:T(8,128)S(1)}, u32[]{:S(2)}, u32[]{:S(2)}) collective-permute-start(f32[2,16,128]{2,1,0:T(8,128)S(1)} %pad_maximum_fusion.5), channel_id=1, source_target_pairs={{48,0},{96,48},{144,96},{192,144},{240,192},{288,240},{336,288},{3... | collective-permute-start | bytes 49160 | tf_op jit(solution)/shard_map/ppermute | solution.py:21
  91.4 15.3 %copy-start.7 = (f32[32,128]{1,0:T(8,128)S(1)}, f32[32,128]{1,0:T(8,128)}, u32[]{:S(2)}) copy-start(f32[32,128]{1,0:T(8,128)} %copy-done.6) | copy-start | bytes 49156
  91.4 15.3 %copy-start.9 = (f32[16]{0:T(128)S(1)}, f32[16]{0:T(128)}, u32[]{:S(2)}) copy-start(f32[16]{0:T(128)} %compare_convert_fusion) | copy-start | bytes 196
  91.9 13.3 %collective-permute-start.6 = (f32[2,16,32]{2,1,0:T(8,128)S(1)}, f32[2,16,32]{2,1,0:T(8,128)S(1)}, u32[]{:S(2)}, u32[]{:S(2)}) collective-permute-start(f32[2,16,32]{2,1,0:T(8,128)S(1)} %pad_maximum_fusion.7), channel_id=1, source_target_pairs={{0,1},{1,2},{2,3},{3,4},{4,5},{5,6},{6,7},{7,8},{8,9},{9,10},{10,1... | collective-permute-start | bytes 12296 | tf_op jit(solution)/shard_map/ppermute | solution.py:21
  94.6 12.0 %collective-permute-start.7 = (f32[2,16,128]{2,1,0:T(8,128)S(1)}, f32[2,16,128]{2,1,0:T(8,128)S(1)}, u32[]{:S(2)}, u32[]{:S(2)}) collective-permute-start(f32[2,16,128]{2,1,0:T(8,128)S(1)} %pad_maximum_fusion.8), channel_id=1, source_target_pairs={{0,48},{48,96},{96,144},{144,192},{192,240},{240,288},{288,336},{3... | collective-permute-start | bytes 49160 | tf_op jit(solution)/shard_map/ppermute | solution.py:21
  108.5 6.5 %collective-permute-start.9 = (f32[2,16,32]{2,1,0:T(8,128)S(1)}, f32[2,16,32]{2,1,0:T(8,128)S(1)}, u32[]{:S(2)}, u32[]{:S(2)}) collective-permute-start(f32[2,16,32]{2,1,0:T(8,128)S(1)} %pad_maximum_fusion.10), channel_id=1, source_target_pairs={{1,0},{2,1},{3,2},{4,3},{5,4},{6,5},{7,6},{8,7},{9,8},{10,9},{11,1... | collective-permute-start | bytes 12296 | tf_op jit(solution)/shard_map/ppermute | solution.py:21
  113.7 11.9 %collective-permute-start.8 = (f32[2,16,128]{2,1,0:T(8,128)S(1)}, f32[2,16,128]{2,1,0:T(8,128)S(1)}, u32[]{:S(2)}, u32[]{:S(2)}) collective-permute-start(f32[2,16,128]{2,1,0:T(8,128)S(1)} %pad_maximum_fusion.9), channel_id=1, source_target_pairs={{48,0},{96,48},{144,96},{192,144},{240,192},{288,240},{336,288},{3... | collective-permute-start | bytes 49160 | tf_op jit(solution)/shard_map/ppermute | solution.py:21
  127.9 13.1 %collective-permute-start.10 = (f32[2,16,32]{2,1,0:T(8,128)S(1)}, f32[2,16,32]{2,1,0:T(8,128)S(1)}, u32[]{:S(2)}, u32[]{:S(2)}) collective-permute-start(f32[2,16,32]{2,1,0:T(8,128)S(1)} %pad_maximum_fusion.11), channel_id=1, source_target_pairs={{0,1},{1,2},{2,3},{3,4},{4,5},{5,6},{6,7},{7,8},{8,9},{9,10},{10,1... | collective-permute-start | bytes 12296 | tf_op jit(solution)/shard_map/ppermute | solution.py:21
  130.0 12.6 %collective-permute-start.11 = (f32[2,16,128]{2,1,0:T(8,128)S(1)}, f32[2,16,128]{2,1,0:T(8,128)S(1)}, u32[]{:S(2)}, u32[]{:S(2)}) collective-permute-start(f32[2,16,128]{2,1,0:T(8,128)S(1)} %pad_maximum_fusion.12), channel_id=1, source_target_pairs={{0,48},{48,96},{96,144},{144,192},{192,240},{240,288},{288,336},{3... | collective-permute-start | bytes 49160 | tf_op jit(solution)/shard_map/ppermute | solution.py:21
  141.5 3.0 %copy-start.13 = (s32[128]{0:T(128)S(1)}, s32[128]{0:T(128)}, u32[]{:S(2)}) copy-start(s32[128]{0:T(128)} %param.11) | copy-start | bytes 1540
  142.7 1.1 copy-start.8
  267.0 2.0 copy-start.3
Sparse Core Ops, SparseCore 0:
  144.6 122.3 all-gather.1
where the time goes:
time: 278 us; the launch traced here: 277 us
  waiting for transfers between devices  145 us (52%)
  starting transfers between devices  71.9 us (26%)
  local copies, waits for them, and re-layouts  29.4 us (11%)
  between operations  14.8 us (5%)
  other arithmetic  12.7 us (5%)
  matrix products  3.83 us (1%)
    all_gather x1, waiting for transfers between devices, on_device(): lax.all_gather(tile, 'xs', axis=1, tiled=True)  119 us
    ppermute x12, starting transfers between devices, from_behind(): return lax.ppermute(block, axis, route)  50.8 us
    ppermute x12, waiting for transfers between devices, from_behind(): return lax.ppermute(block, axis, route)  19.8 us
    all_to_all x1, starting transfers between devices, on_device(): lax.all_to_all(out_rows, 'ys', split_axis=0, concat_axis=0, tiled=True)  15.6 us
    slice x17, local copies, waits for them, and re-layouts, along_next(): lax.slice_in_dim(inner, 1, inner.shape[axis], axis=axis)  7.26 us
  transfers between devices with their start and end apart: 15, of which 6 were waited for; matrix products, arithmetic and copies ran while one was open for 11% of the time, Pallas kernels for 0%

commit v1 on v0

v1 whole, which is shorter than its diff:
```python
import math

import jax
import jax.numpy as jnp
from jax import lax
from jax.experimental import pallas as pl
from jax.experimental.pallas import tpu as pltpu
from jax.sharding import PartitionSpec as P

GRID_X = 5000
X0 = 2000
ZS = 8
DT = 0.5
NXS = 16
NYS = 48
NZ = 16
CX = 32
RX = 40
LANES = 128
HI = lax.Precision.HIGHEST

FROM_PREV = (
    [(k, r) for k in (0, 1, 2, 4, 5) for r in (29, 30, 31)]
    + [(3, 30), (3, 31)]
    + [(6, 30), (6, 31)]
)
FROM_NEXT = (
    [(k, r) for k in (1, 2) for r in (0, 1, 2)]
    + [(k, r) for k in (0, 3, 4, 5) for r in (0, 1)]
    + [(6, 0), (6, 1)]
)
NLO = len(FROM_PREV)
NHI = len(FROM_NEXT)
EARLY = 5


def rows_of(boxes):
    found, at = [], 0
    for comps, r, first, count in boxes:
        for k in comps:
            found.append((k, r, first, count, at))
            at += count
    return found, at


ALL = tuple(range(7))
TILE_PREV, TLO = rows_of(((ALL, 31, 6, 5), (ALL, 30, 7, 3), ((0, 1, 5), 29, 8, 1)))
TILE_NEXT, THI = rows_of(((ALL, 0, 5, 6), (ALL, 1, 6, 4), ((1, 2), 2, 7, 2)))


def iota(shape, axis):
    return lax.broadcasted_iota(jnp.int32, shape, axis)


def half_h(e, h, dt, ops):
    ex, ey, ez = e
    hx, hy, hz = h
    xn, yn, zn = ops
    hx2 = hx - dt * ((yn(ez, 1) - ez) - (zn(ey, 1) - ey))
    hy2 = hy - dt * ((zn(ex, 0) - ex) - (xn(ez) - ez))
    hz2 = hz - dt * ((xn(ey) - ey) - (yn(ex, 0) - ex))
    return hx2, hy2, hz2


def half_e(e, h, c, source, ops):
    ex, ey, ez = e
    hx, hy, hz = h
    xp, yp, zp = ops
    ex2 = ex + c * ((hz - yp(hz, 1)) - (hy - zp(hy, 1)))
    ey2 = ey + c * ((hx - zp(hx, 0)) - (hz - xp(hz)))
    ez2 = ez + c * ((hy - xp(hy)) - (hx - yp(hx, 0)) - source)
    return ex2, ey2, ez2


def kernel(
    fields_ref, perm_ref, adj_ref, owner_ref, row_ref, angle_ref,
    newf_ref, far_ref,
    fld, tmp, strip, own_p, own_p4, in_p, in_p4, ye, yh, dtf, dts,
    send_lo, send_hi, recv_lo, recv_hi, tsend_lo, tsend_hi, trecv_lo, trecv_hi,
    outbox, inbox, cur, cur_p, in_sx, in_sp, in_sd, src_s,
    tiles, weights, zsend, zrecv,
    load_sem, a_send, a_recv, x_send, x_recv, p_send, p_recv, p4_send, p4_recv,
    s_send, s_recv, t_send, t_recv, z_send, z_recv,
):
    mx = lax.axis_index("xs")
    my = lax.axis_index("ys")
    xn_dev = lax.rem(mx + 1, NXS)
    xp_dev = lax.rem(mx + NXS - 1, NXS)
    yn_dev = lax.rem(my + 1, NYS)
    yp_dev = lax.rem(my + NYS - 1, NYS)
    ring = mx // 2
    zh = lax.rem(mx, 2)
    partner = ring * 2 + (1 - zh)
    m_xlo = jnp.where(mx == 0, 0.0, 1.0)
    m_xhi = jnp.where(mx == NXS - 1, 0.0, 1.0)
    m_ylo = jnp.where(my == 0, 0.0, 1.0)
    m_yhi = jnp.where(my == NYS - 1, 0.0, 1.0)

    def remote(src, dst, ssem, rsem, dev):
        return pltpu.make_async_remote_copy(
            src_ref=src, dst_ref=dst, send_sem=ssem, recv_sem=rsem,
            device_id=dev, device_id_type=pl.DeviceIdType.MESH,
        )

    inbox[...] = jnp.zeros(inbox.shape, jnp.float32)
    bar = pltpu.get_barrier_semaphore()

    def greet(dev):
        pl.semaphore_signal(bar, inc=1, device_id=dev, device_id_type=pl.DeviceIdType.MESH)

    near = [
        (xn_dev, my), (xp_dev, my),
        (xn_dev, yn_dev), (xn_dev, yp_dev), (xp_dev, yn_dev), (xp_dev, yp_dev),
    ] + [(lax.rem(ring + d, 8) * 2 + zh, my) for d in range(1, 8)]
    for dev in near:
        greet(dev)

    @pl.loop(1, NYS)
    def _(d):
        greet((mx, lax.rem(my + d, NYS)))

    load_f = pltpu.make_async_copy(
        fields_ref, fld.at[pl.ds(0, 6), pl.ds(1, NZ), pl.ds(0, CX), :], load_sem.at[0]
    )
    load_c = pltpu.make_async_copy(
        perm_ref, fld.at[6, pl.ds(1, NZ), pl.ds(0, CX), :], load_sem.at[1]
    )
    load_f.start()
    load_c.start()

    n_adj = adj_ref.shape[0]
    own_row = owner_ref[...].astype(jnp.float32)
    ii = iota((n_adj, n_adj), 0)
    jj = iota((n_adj, n_adj), 1)
    own_b = jnp.broadcast_to(own_row, (n_adj, n_adj))
    row_b = jnp.broadcast_to(row_ref[...].astype(jnp.float32), (n_adj, n_adj))
    own_col = jnp.sum(jnp.where(ii == jj, own_b, 0.0), axis=1, keepdims=True)
    row_col = jnp.sum(jnp.where(ii == jj, row_b, 0.0), axis=1, keepdims=True)
    same = own_col == own_b
    rank_row = jnp.sum(jnp.where(same & (ii < jj), 1.0, 0.0), axis=0, keepdims=True)
    rank_col = jnp.sum(jnp.where(same & (jj < ii), 1.0, 0.0), axis=1, keepdims=True)
    place = iota((NYS * 8, n_adj), 0).astype(jnp.float32)
    pick_val = jnp.where(place == own_row * 8.0 + rank_row, 1.0, 0.0)
    pick_row = jnp.where(place == own_row * 8.0 + 4.0, 1.0, 0.0)
    lane_f = iota((n_adj, LANES), 1).astype(jnp.float32)
    base = (lax.rem(my, 16) * 8).astype(jnp.float32)
    row_at = jnp.where(lane_f == base + rank_col, row_col + 1.0, 0.0)
    out = jnp.dot(pick_val, adj_ref[...], precision=HI, preferred_element_type=jnp.float32)
    out = out + jnp.dot(pick_row, row_at, precision=HI, preferred_element_type=jnp.float32)
    outbox[...] = out.reshape(NYS, 8, LANES)

    lane = iota((8, LANES), 1)
    for k in range(7):
        for z in range(NZ + 2):
            fld[k, z, pl.ds(CX, 8), :] = jnp.zeros((8, LANES), jnp.float32)
        for z in (0, NZ + 1):
            fld[k, z, pl.ds(0, CX), :] = jnp.zeros((CX, LANES), jnp.float32)
    for k in (3, 4):
        tmp[k, 5, :, :] = jnp.zeros((RX, LANES), jnp.float32)
    r40 = iota((RX, LANES), 0)
    row_m = jnp.where(
        r40 < CX, 1.0, jnp.where(r40 < CX + 3, m_xhi, jnp.where(r40 >= RX - 3, m_xlo, 0.0))
    )
    dtf[...] = DT * row_m
    slot40 = iota((RX, LANES), 1) & 7
    dts[0] = DT * row_m * jnp.where(slot40 < 3, m_ylo, jnp.where(slot40 < 6, 1.0, 0.0))
    dts[1] = DT * row_m * jnp.where(slot40 < 3, 1.0, jnp.where(slot40 < 6, m_yhi, 0.0))

    load_f.wait()
    load_c.wait()

    @pl.loop(1, NZ + 1)
    def _(z):
        fld[6, z, pl.ds(0, CX), :] = DT / fld[6, z, pl.ds(0, CX), :]

    flat = fld.reshape(7 * (NZ + 2) * RX, LANES)

    def rows_at(k, z, r, n):
        return pl.ds((k * (NZ + 2) + z + 1) * RX + r, n, stride=RX)

    def pack_x(send, rows, early, early_rows):
        for k, r, z, n, at in early_rows:
            early[pl.ds(at, n), :] = flat[rows_at(k, z, r, n), :]
        for i, (k, r) in enumerate(rows):
            send[i, :, :] = flat[rows_at(k, 0, r, NZ), :]

    pack_x(send_lo, FROM_PREV, tsend_lo, TILE_PREV)
    pack_x(send_hi, FROM_NEXT, tsend_hi, TILE_NEXT)

    def pack_strip(load, n):
        lanes = iota((n, LANES), 1)
        total = jnp.zeros((n, LANES), jnp.float32)
        for z in range(NZ):
            turned = pltpu.roll(load(z), 8 * z + 3, 1)
            total = jnp.where((lanes >> 3) == z, turned, total)
        return jnp.where((lanes & 7) < 6, total, 0.0)

    @pl.loop(0, 7)
    def _(k):
        own_p[k, :, :] = pack_strip(lambda z: fld[k, z + 1, pl.ds(0, CX), :], CX)

    r32 = iota((32, LANES), 0)
    owner_xs = jnp.where(r32 < 16, ring * 2 + zh, ring * 2 + (1 - zh))
    a_index = owner_xs * 8 + ((r32 & 15) >> 1)
    angle_row = jnp.broadcast_to(angle_ref[...].astype(jnp.float32), (32, LANES))
    wave = jnp.sum(
        jnp.where(iota((32, LANES), 1) == a_index, angle_row, 0.0), axis=1, keepdims=True
    )
    col = iota((32, 8 * CX), 1)
    x_pos = ((col >> 5) * 2 + zh) * CX + (col & 31) + X0
    prod = wave * x_pos.astype(jnp.float32)
    turn = prod - jnp.floor(prod * (1.0 / GRID_X)) * float(GRID_X)
    turn = jnp.where(turn < 0.0, turn + float(GRID_X), turn)
    turn = jnp.where(turn >= float(GRID_X), turn - float(GRID_X), turn)
    quad = jnp.floor(turn * (4.0 / GRID_X) + 0.5)
    th = (turn - quad * (GRID_X / 4.0)) * (2.0 * math.pi / GRID_X)
    t2 = th * th
    sn = th * (1.0 + t2 * (-1.0 / 6 + t2 * (1.0 / 120 + t2 * (-1.0 / 5040 + t2 * (1.0 / 362880)))))
    cs = 1.0 + t2 * (-0.5 + t2 * (1.0 / 24 + t2 * (-1.0 / 720 + t2 * (1.0 / 40320 - t2 * (1.0 / 3628800)))))
    odd = (quad == 1.0) | (quad == 3.0)
    c_abs = jnp.where(odd, sn, cs)
    s_abs = jnp.where(odd, cs, sn)
    cosine = jnp.where((quad == 1.0) | (quad == 2.0), -c_abs, c_abs)
    sine = jnp.where((quad == 2.0) | (quad == 3.0), -s_abs, s_abs)
    scale = 1.0 / math.sqrt(NXS * CX)
    is_re = (iota((32, 8 * CX), 0) & 1) == 0
    weights[...] = jnp.where(is_re, cosine, -sine) * scale

    pl.semaphore_wait(bar, len(near) + NYS - 1)

    def a_copy(d):
        to = lax.rem(my + d, NYS)
        return remote(
            outbox.at[to, pl.ds(0, 5), :], inbox.at[my, pl.ds(0, 5), :],
            a_send.at[d], a_recv.at[my], (mx, to),
        )

    @pl.loop(1, NYS)
    def _(d):
        a_copy(d).start()

    def x_copies(i, part, count):
        lo, hi = pl.ds(part, count or NLO - part), pl.ds(part, count or NHI - part)
        return [
            remote(send_lo.at[lo], recv_lo.at[lo], x_send.at[i, 0], x_recv.at[i, 0], (xn_dev, my)),
            remote(send_hi.at[hi], recv_hi.at[hi], x_send.at[i, 1], x_recv.at[i, 1], (xp_dev, my)),
        ]

    x_first = [
        remote(tsend_lo, trecv_lo, x_send.at[0, 0], x_recv.at[0, 0], (xn_dev, my)),
        remote(tsend_hi, trecv_hi, x_send.at[0, 1], x_recv.at[0, 1], (xp_dev, my)),
    ]
    x_early = x_copies(1, 0, EARLY)
    for c in x_first:
        c.start()
    p_copies = [
        remote(own_p, in_p.at[0], p_send.at[0], p_recv.at[0], (mx, yn_dev)),
        remote(own_p, in_p.at[1], p_send.at[1], p_recv.at[1], (mx, yp_dev)),
    ]
    for c in p_copies + x_early:
        c.start()

    inbox[my] = outbox[my]

    @pl.loop(1, NYS)
    def _(d):
        frm = lax.rem(my + d, NYS)
        remote(
            outbox.at[frm, pl.ds(0, 5), :], inbox.at[frm, pl.ds(0, 5), :],
            a_send.at[d], a_recv.at[frm], (mx, frm),
        ).wait_recv()

    current = jnp.zeros((CX, LANES), jnp.float32)
    x_id = (iota((CX, LANES), 0) + 1).astype(jnp.float32)
    for q in range(3):
        block = inbox[pl.ds(16 * q, 16), :, :]
        ids = jnp.sum(inbox[pl.ds(16 * q, 16), 4, :], axis=0, keepdims=True)
        landing = jnp.where(x_id == ids, 1.0, 0.0)
        current = current + jnp.dot(
            landing, block.reshape(16 * 8, LANES), precision=HI, preferred_element_type=jnp.float32
        )
    cur[pl.ds(0, CX), :] = current

    def pack_s(v):
        lanes = iota(v.shape, 1)
        inside = (lanes >= 8 * ZS) & (lanes < 8 * ZS + 6)
        return jnp.where(inside, pltpu.roll(v, 8 * ZS + 3, 1), 0.0)

    cur_p[pl.ds(0, CX), :] = pack_s(current)
    lo8 = pl.ds(0, 8)
    hi8 = pl.ds(CX - 8, 8)
    s_copies = [
        remote(cur.at[hi8, :], in_sx.at[0], s_send.at[0], s_recv.at[0], (xn_dev, my)),
        remote(cur.at[lo8, :], in_sx.at[1], s_send.at[1], s_recv.at[1], (xp_dev, my)),
        remote(cur_p.at[hi8, :], in_sd.at[0, 0], s_send.at[2], s_recv.at[2], (xn_dev, yn_dev)),
        remote(cur_p.at[hi8, :], in_sd.at[0, 1], s_send.at[3], s_recv.at[3], (xn_dev, yp_dev)),
        remote(cur_p.at[lo8, :], in_sd.at[1, 0], s_send.at[4], s_recv.at[4], (xp_dev, yn_dev)),
        remote(cur_p.at[lo8, :], in_sd.at[1, 1], s_send.at[5], s_recv.at[5], (xp_dev, yp_dev)),
        remote(cur_p.at[pl.ds(0, CX), :], in_sp.at[0], s_send.at[6], s_recv.at[6], (mx, yn_dev)),
        remote(cur_p.at[pl.ds(0, CX), :], in_sp.at[1], s_send.at[7], s_recv.at[7], (mx, yp_dev)),
    ]
    for c in s_copies:
        c.start()
    x_second = x_copies(2, EARLY, 0)
    for c in x_second:
        c.start()

    def unpack_x(recv, rows, early, early_rows, base, mask):
        for k, r, z, n, at in early_rows:
            flat[rows_at(k, z, r + base, n), :] = early[pl.ds(at, n), :] * mask
        for i, (k, r) in enumerate(rows):
            flat[rows_at(k, 0, r + base, NZ), :] = recv[i, :, :] * mask

    def p4_copies(part):
        return [
            remote(own_p4.at[part], in_p4.at[part, 0], p4_send.at[part, 0], p4_recv.at[part, 0], (mx, yn_dev)),
            remote(own_p4.at[part], in_p4.at[part, 1], p4_send.at[part, 1], p4_recv.at[part, 1], (mx, yp_dev)),
        ]

    def halo_in(part, copies):
        for c in copies:
            c.wait_recv()
        if part == 0:
            unpack_x(None, (), trecv_lo, TILE_PREV, 8, m_xlo)
            unpack_x(None, (), trecv_hi, TILE_NEXT, CX, m_xhi)
        else:
            unpack_x(recv_lo, FROM_PREV, None, (), 8, m_xlo)
            unpack_x(recv_hi, FROM_NEXT, None, (), CX, m_xhi)

        @pl.loop(0, 7)
        def _(k):
            own_p4[part, k, :, :] = pack_strip(lambda z: fld[k, z + 1, pl.ds(CX, 8), :], 8)

        sent = p4_copies(part)
        for c in sent:
            c.start()
        return sent

    def build_strips(part):
        @pl.loop(0, 7)
        def _(k):
            for rows, own, got in (
                (pl.ds(0, CX), own_p[k], (in_p[0, k], in_p[1, k])),
                (pl.ds(CX, 8), own_p4[part, k], (in_p4[part, 0, k], in_p4[part, 1, k])),
            ):
                low = (iota(own.shape, 1) & 7) < 3
                strip[0, k, rows, :] = jnp.where(low, got[0] * m_ylo, own)
                strip[1, k, rows, :] = jnp.where(low, own, got[1] * m_yhi)

    lane40 = iota((RX, LANES), 1)

    def x_next(v):
        return pltpu.roll(v, RX - 1, 0)

    def x_prev(v):
        return pltpu.roll(v, 1, 0)

    def strips_run():
        def zn(v, _):
            return jnp.where(lane40 < 8 * (NZ - 1), pltpu.roll(v, LANES - 8, 1), 0.0)

        def zp(v, _):
            return jnp.where(lane40 >= 8, pltpu.roll(v, 8, 1), 0.0)

        def yn(v, _):
            return pltpu.roll(v, LANES - 1, 1)

        def yp(v, _):
            return pltpu.roll(v, 1, 1)

        for step in range(3):
            for side in range(2):
                e = [strip[side, k] for k in range(3)]
                if side == 1:
                    ye[step, 0, :, :] = e[0]
                    ye[step, 1, :, :] = e[2]
                    if step == 2:
                        continue
                h = [strip[side, k] for k in range(3, 6)]
                h = half_h(e, h, dts[side], (x_next, yn, zn))
                if side == 0:
                    yh[step, 0, :, :] = h[0]
                    yh[step, 1, :, :] = h[2]
                    if step == 2:
                        continue
                e = half_e(e, h, strip[side, 6], src_s[side], (x_prev, yp, zp))
                for k in range(3):
                    strip[side, k, :, :] = e[k]
                    strip[side, 3 + k, :, :] = h[k]

    def sweep(step, src, dst, first, last):
        @pl.loop(first, last + 1)
        def _(z):
            sh_e = lax.rem(124 - 8 * (z - 1) + 128, 128)
            sh_h = lax.rem(126 - 8 * (z - 1) + 128, 128)
            dt = dtf[...]
            e = [src[k, z] for k in range(3)]
            h = [src[k, z] for k in range(3, 6)]

            def yn(v, i):
                edge = pltpu.roll(ye[step, i], sh_e, 1)
                return jnp.where(lane40 == LANES - 1, edge, pltpu.roll(v, LANES - 1, 1))

            def zn(v, i):
                return src[i, z + 1]

            def yp(v, i):
                edge = pltpu.roll(yh[step, i], sh_h, 1)
                return jnp.where(lane40 == 0, edge, pltpu.roll(v, 1, 1))

            def zp(v, i):
                return dst[3 + i, z - 1]

            h = half_h(e, h, dt, (x_next, yn, zn))
            on = jnp.where(z == ZS + 1, 1.0, 0.0)
            e = half_e(e, h, fld[6, z], cur[...] * on, (x_prev, yp, zp))
            for k in range(3):
                dst[k, z] = e[k]
                dst[3 + k, z] = h[k]

    p4_first = halo_in(0, x_first)
    for c in p_copies:
        c.wait_recv()
    for c in p4_first:
        c.wait_recv()
    build_strips(0)
    for c in s_copies:
        c.wait_recv()
    r8 = iota((8, LANES), 0)

    def tile4(lo, hi):
        return jnp.where(r8 < 3, hi * m_xhi, jnp.where(r8 >= 5, lo * m_xlo, 0.0))

    cur4 = tile4(in_sx[0], in_sx[1])
    cur[pl.ds(CX, 8), :] = cur4
    own4 = pack_s(cur4)
    low32 = (iota((CX, LANES), 1) & 7) < 3
    low8 = (lane & 7) < 3
    own32 = cur_p[pl.ds(0, CX), :]
    src_s[0, pl.ds(0, CX), :] = jnp.where(low32, in_sp[0] * m_ylo, own32)
    src_s[1, pl.ds(0, CX), :] = jnp.where(low32, own32, in_sp[1] * m_yhi)
    src_s[0, pl.ds(CX, 8), :] = jnp.where(low8, tile4(in_sd[0, 0], in_sd[1, 0]) * m_ylo, own4)
    src_s[1, pl.ds(CX, 8), :] = jnp.where(low8, own4, tile4(in_sd[0, 1], in_sd[1, 1]) * m_yhi)

    strips_run()
    sweep(0, fld, tmp, 6, 11)
    sweep(1, tmp, tmp, 7, 10)
    sweep(2, tmp, tmp, 8, 9)
    own_x = pl.ds(0, CX)
    mine = pl.ds(ring * CX, CX)
    tiles[0, mine, :] = -tmp[4, ZS + 1, own_x, :]
    tiles[1, mine, :] = tmp[3, ZS + 1, own_x, :]
    tiles[2, mine, :] = tmp[1, ZS + 1, own_x, :]
    tiles[3, mine, :] = -tmp[0, ZS + 1, own_x, :]

    def t_copy(d, c, whose):
        at = pl.ds(pl.multiple_of(whose * CX, CX), CX)
        to = lax.rem(ring + d, 8) * 2 + zh
        return remote(
            tiles.at[c, at, :], tiles.at[c, at, :],
            t_send.at[d - 1, c], t_recv.at[d - 1, c], (to, my),
        )

    for c in range(4):
        for d in (4, 3, 5, 2, 6, 1, 7):
            t_copy(d, c, ring).start()

    p4_second = halo_in(1, x_early + x_second)

    z_copies = []
    for c in range(4):
        for d in range(1, 8):
            t_copy(d, c, lax.rem(ring + 8 - d, 8)).wait_recv()
        zsend[c, :, :] = jnp.dot(
            weights[...], tiles[c], precision=HI, preferred_element_type=jnp.float32
        )
        copy = remote(zsend.at[c, pl.ds(16, 16), :], zrecv.at[c], z_send.at[c], z_recv.at[c], (partner, my))
        copy.start()
        z_copies.append(copy)

    for c in p4_second:
        c.wait_recv()
    build_strips(1)
    strips_run()
    for step in range(3):
        sweep(step, fld, fld, 1, NZ)
    store = pltpu.make_async_copy(
        fld.at[pl.ds(0, 6), pl.ds(1, NZ), pl.ds(0, CX), :], newf_ref, load_sem.at[2]
    )
    store.start()

    for c in range(4):
        z_copies[c].wait_recv()
        far_ref[pl.ds(c, 16, stride=4), :] = zsend[c, pl.ds(0, 16), :] + zrecv[c]

    @pl.loop(1, NYS)
    def _(d):
        a_copy(d).wait_send()

    for c in x_first + x_early + x_second + p_copies + p4_first + p4_second + s_copies + z_copies:
        c.wait_send()
    for c in range(4):
        for d in range(1, 8):
            t_copy(d, c, ring).wait_send()
    store.wait()


def on_device(fields, permittivity, adj_values, adj_owner, adj_row, angle_wave):
    n_adj = adj_values.shape[0]
    f32 = jnp.float32
    vmem = lambda *shape: pltpu.VMEM(shape, f32)
    dma = pltpu.SemaphoreType.DMA
    whole = pl.BlockSpec(memory_space=pltpu.VMEM)
    anywhere = pl.BlockSpec(memory_space=pl.ANY)
    new_fields, far = pl.pallas_call(
        kernel,
        out_shape=(
            jax.ShapeDtypeStruct(fields.shape, f32),
            jax.ShapeDtypeStruct((64, LANES), f32),
        ),
        in_specs=[anywhere, anywhere, whole, whole, whole, whole],
        out_specs=(anywhere, whole),
        scratch_shapes=[
            vmem(7, NZ + 2, RX, LANES),
            vmem(6, NZ + 2, RX, LANES),
            vmem(2, 7, RX, LANES),
            vmem(7, CX, LANES),
            vmem(2, 7, 8, LANES),
            vmem(2, 7, CX, LANES),
            vmem(2, 2, 7, 8, LANES),
            vmem(3, 2, RX, LANES),
            vmem(3, 2, RX, LANES),
            vmem(RX, LANES),
            vmem(2, RX, LANES),
            vmem(NLO, NZ, LANES),
            vmem(NHI, NZ, LANES),
            vmem(NLO, NZ, LANES),
            vmem(NHI, NZ, LANES),
            vmem(TLO, LANES),
            vmem(THI, LANES),
            vmem(TLO, LANES),
            vmem(THI, LANES),
            vmem(NYS, 8, LANES),
            vmem(NYS, 8, LANES),
            vmem(RX, LANES),
            vmem(RX, LANES),
            vmem(2, 8, LANES),
            vmem(2, CX, LANES),
            vmem(2, 2, 8, LANES),
            vmem(2, RX, LANES),
            vmem(4, 8 * CX, LANES),
            vmem(32, 8 * CX),
            vmem(4, 32, LANES),
            vmem(4, 16, LANES),
            dma((3,)),
            dma((NYS,)),
            dma((NYS,)),
            dma((3, 2)),
            dma((3, 2)),
            dma((2,)),
            dma((2,)),
            dma((2, 2)),
            dma((2, 2)),
            dma((8,)),
            dma((8,)),
            dma((7, 4)),
            dma((7, 4)),
            dma((4,)),
            dma((4,)),
        ],
        compiler_params=pltpu.CompilerParams(collective_id=1, has_side_effects=True),
        name="fdtd_far_field",
    )(
        fields,
        permittivity,
        adj_values,
        adj_owner.reshape(1, n_adj),
        adj_row.reshape(1, n_adj),
        angle_wave.reshape(1, angle_wave.shape[0]),
    )
    return new_fields, far.reshape(8, 2, 4, LANES)


def solution(mesh):
    placed = (
        P(None, None, "xs", "ys"),
        P(None, "xs", "ys"),
        P(("xs", "ys"), None),
        P(("xs", "ys"), None),
        P(("xs", "ys")),
        P(),
    )
    return jax.shard_map(
        on_device,
        mesh=mesh,
        in_specs=placed,
        out_specs=(P(None, None, "xs", "ys"), P("xs", None, None, "ys")),
        check_vma=False,
    )
```

time: 278 us -> 89.2 us (0.32)
  the two profiles are of different devices: /device:TPU:2 before, /device:TPU:8 now
where the time goes in v1:
time: 89.2 us; the launch traced here: 89 us
  Pallas kernels  84.9 us (95%)
  local copies, waits for them, and re-layouts  3.38 us (4%)
    pallas_call x1, Pallas kernels, on_device(): pl.pallas_call(kernel, out_shape=(jax.ShapeDtypeStruct(fields.shape, f32)...  84.9 us
    unnamed x4, local copies, waits for them, and re-layouts  3.38 us

profile of v1, /device:TPU:8, one launch (start us, length us, event | category | flops | bytes accessed | tf_op | source)
XLA Modules:
  0.0 89.0 jit_solution(6778123995852435299)
XLA Ops:
  0.6 84.9 %fdtd_far_field.1 = (f32[6,16,32,128]{3,2,1,0:T(8,128)}, f32[64,128]{1,0:T(8,128)}) custom-call(f32[6,16,32,128]{3,2,1,0:T(8,128)} %fields_ref.1, f32[16,32,128]{2,1,0:T(8,128)} %perm_ref.1, f32[96,128]{1,0:T(8,128)} %adj_ref.1, s32[1,96]{1,0:T(1,128)} %bitcast.5, s32[1,96]{1,0:T(1,128)} %bitcast.6, s32[1,128]{1,0:T(1,128)} %bitcast.7), custom_call_target="tpu_custom_call" | custom-call | tf_op jit(solution)/shard_map/fdtd_far_field/pallas_call | solution.py:515
  85.6 0.0 copy-start
  85.6 2.8 %copy.10 = f32[6,16,32,128]{3,2,1,0:T(8,128)} copy(f32[6,16,32,128]{3,2,1,0:T(8,128)} %get-tuple-element.8) | data formatting | bytes 3145728
  88.3 0.0 copy-done
  88.3 0.6 copy.11
Async XLA Ops:
  85.6 2.8 %copy-start = (f32[64,128]{1,0:T(8,128)S(1)}, f32[64,128]{1,0:T(8,128)}, u32[]{:S(2)}) copy-start(f32[64,128]{1,0:T(8,128)} %get-tuple-element.5) | copy-start | bytes 98308

commit v2 on v1

--- a/solution.py
+++ b/solution.py
@@ -29,23 +29,31 @@
     + [(k, r) for k in (0, 3, 4, 5) for r in (0, 1)]
     + [(6, 0), (6, 1)]
 )
-NLO = len(FROM_PREV)
-NHI = len(FROM_NEXT)
-EARLY = 5
-
-
-def rows_of(boxes):
-    found, at = [], 0
-    for comps, r, first, count in boxes:
-        for k in comps:
-            found.append((k, r, first, count, at))
-            at += count
-    return found, at
-
-
 ALL = tuple(range(7))
-TILE_PREV, TLO = rows_of(((ALL, 31, 6, 5), (ALL, 30, 7, 3), ((0, 1, 5), 29, 8, 1)))
-TILE_NEXT, THI = rows_of(((ALL, 0, 5, 6), (ALL, 1, 6, 4), ((1, 2), 2, 7, 2)))
+EARLY = 2
+
+
+def split_halo(slabs, boxes):
+    inner = {(k, r): (z, n) for comps, r, z, n in boxes for k in comps}
+    tile = [(k, r, z, n) for (k, r), (z, n) in inner.items()]
+    outer = ([], [])
+    for i, (k, r) in enumerate(slabs):
+        z, n = inner.get((k, r), (NZ, 0))
+        outer[i >= EARLY].append((k, r, 0, z))
+        if z + n < NZ:
+            outer[i >= EARLY].append((k, r, z + n, NZ - z - n))
+    parts = []
+    for entries in (tile, *outer):
+        placed, at = [], 0
+        for k, r, z, n in entries:
+            placed.append((k, r, z, n, at))
+            at += n
+        parts.append((placed, at))
+    return parts
+
+
+PARTS_LO = split_halo(FROM_PREV, ((ALL, 31, 6, 5), (ALL, 30, 7, 3), ((0, 1, 5), 29, 8, 1)))
+PARTS_HI = split_halo(FROM_NEXT, ((ALL, 0, 5, 6), (ALL, 1, 6, 4), ((1, 2), 2, 7, 2)))
 
 
 def iota(shape, axis):
@@ -76,12 +84,15 @@
     fields_ref, perm_ref, adj_ref, owner_ref, row_ref, angle_ref,
     newf_ref, far_ref,
     fld, tmp, strip, own_p, own_p4, in_p, in_p4, ye, yh, dtf, dts,
-    send_lo, send_hi, recv_lo, recv_hi, tsend_lo, tsend_hi, trecv_lo, trecv_hi,
+    send_lo0, send_lo1, send_lo2, send_hi0, send_hi1, send_hi2,
+    recv_lo0, recv_lo1, recv_lo2, recv_hi0, recv_hi1, recv_hi2,
     outbox, inbox, cur, cur_p, in_sx, in_sp, in_sd, src_s,
     tiles, weights, zsend, zrecv,
     load_sem, a_send, a_recv, x_send, x_recv, p_send, p_recv, p4_send, p4_recv,
     s_send, s_recv, t_send, t_recv, z_send, z_recv,
 ):
+    send_lo, send_hi = (send_lo0, send_lo1, send_lo2), (send_hi0, send_hi1, send_hi2)
+    recv_lo, recv_hi = (recv_lo0, recv_lo1, recv_lo2), (recv_hi0, recv_hi1, recv_hi2)
     mx = lax.axis_index("xs")
     my = lax.axis_index("ys")
     xn_dev = lax.rem(mx + 1, NXS)
@@ -155,8 +166,8 @@
             fld[k, z, pl.ds(CX, 8), :] = jnp.zeros((8, LANES), jnp.float32)
         for z in (0, NZ + 1):
             fld[k, z, pl.ds(0, CX), :] = jnp.zeros((CX, LANES), jnp.float32)
-    for k in (3, 4):
-        tmp[k, 5, :, :] = jnp.zeros((RX, LANES), jnp.float32)
+    for k, z in ((3, 5), (4, 5), (3, 0), (4, 0), (0, NZ + 1), (1, NZ + 1)):
+        tmp[k, z, :, :] = jnp.zeros((RX, LANES), jnp.float32)
     r40 = iota((RX, LANES), 0)
     row_m = jnp.where(
         r40 < CX, 1.0, jnp.where(r40 < CX + 3, m_xhi, jnp.where(r40 >= RX - 3, m_xlo, 0.0))
@@ -178,14 +189,10 @@
     def rows_at(k, z, r, n):
         return pl.ds((k * (NZ + 2) + z + 1) * RX + r, n, stride=RX)
 
-    def pack_x(send, rows, early, early_rows):
-        for k, r, z, n, at in early_rows:
-            early[pl.ds(at, n), :] = flat[rows_at(k, z, r, n), :]
-        for i, (k, r) in enumerate(rows):
-            send[i, :, :] = flat[rows_at(k, 0, r, NZ), :]
-
-    pack_x(send_lo, FROM_PREV, tsend_lo, TILE_PREV)
-    pack_x(send_hi, FROM_NEXT, tsend_hi, TILE_NEXT)
+    for sends, parts in ((send_lo, PARTS_LO), (send_hi, PARTS_HI)):
+        for send, (entries, _) in zip(sends, parts):
+            for k, r, z, n, at in entries:
+                send[pl.ds(at, n), :] = flat[rows_at(k, z, r, n), :]
 
     def pack_strip(load, n):
         lanes = iota((n, LANES), 1)
@@ -239,18 +246,13 @@
     def _(d):
         a_copy(d).start()
 
-    def x_copies(i, part, count):
-        lo, hi = pl.ds(part, count or NLO - part), pl.ds(part, count or NHI - part)
+    def x_copies(i):
         return [
-            remote(send_lo.at[lo], recv_lo.at[lo], x_send.at[i, 0], x_recv.at[i, 0], (xn_dev, my)),
-            remote(send_hi.at[hi], recv_hi.at[hi], x_send.at[i, 1], x_recv.at[i, 1], (xp_dev, my)),
+            remote(send_lo[i], recv_lo[i], x_send.at[i, 0], x_recv.at[i, 0], (xn_dev, my)),
+            remote(send_hi[i], recv_hi[i], x_send.at[i, 1], x_recv.at[i, 1], (xp_dev, my)),
         ]
 
-    x_first = [
-        remote(tsend_lo, trecv_lo, x_send.at[0, 0], x_recv.at[0, 0], (xn_dev, my)),
-        remote(tsend_hi, trecv_hi, x_send.at[0, 1], x_recv.at[0, 1], (xp_dev, my)),
-    ]
-    x_early = x_copies(1, 0, EARLY)
+    x_first, x_early, x_second = x_copies(0), x_copies(1), x_copies(2)
     for c in x_first:
         c.start()
     p_copies = [
@@ -301,15 +303,13 @@
     ]
     for c in s_copies:
         c.start()
-    x_second = x_copies(2, EARLY, 0)
-    for c in x_second:
-        c.start()
-
-    def unpack_x(recv, rows, early, early_rows, base, mask):
-        for k, r, z, n, at in early_rows:
-            flat[rows_at(k, z, r + base, n), :] = early[pl.ds(at, n), :] * mask
-        for i, (k, r) in enumerate(rows):
-            flat[rows_at(k, 0, r + base, NZ), :] = recv[i, :, :] * mask
+
+    def unpack_x(i):
+        for recv, parts, base, mask in (
+            (recv_lo, PARTS_LO, 8, m_xlo), (recv_hi, PARTS_HI, CX, m_xhi)
+        ):
+            for k, r, z, n, at in parts[i][0]:
+                flat[rows_at(k, z, r + base, n), :] = recv[i][pl.ds(at, n), :] * mask
 
     def p4_copies(part):
         return [
@@ -320,12 +320,8 @@
     def halo_in(part, copies):
         for c in copies:
             c.wait_recv()
-        if part == 0:
-            unpack_x(None, (), trecv_lo, TILE_PREV, 8, m_xlo)
-            unpack_x(None, (), trecv_hi, TILE_NEXT, CX, m_xhi)
-        else:
-            unpack_x(recv_lo, FROM_PREV, None, (), 8, m_xlo)
-            unpack_x(recv_hi, FROM_NEXT, None, (), CX, m_xhi)
+        for i in (0,) if part == 0 else (1, 2):
+            unpack_x(i)
 
         @pl.loop(0, 7)
         def _(k):
@@ -388,35 +384,58 @@
                     strip[side, k, :, :] = e[k]
                     strip[side, 3 + k, :, :] = h[k]
 
-    def sweep(step, src, dst, first, last):
+    def sweep(step, src, dst, first, last, rows, keep=None):
+        height = sum(n for _, n in rows)
+        lanes = iota((height, LANES), 1)
+
+        def take(ref, *at):
+            got = [ref[(*at, pl.ds(r, n), slice(None))] for r, n in rows]
+            return got[0] if len(got) == 1 else jnp.concatenate(got, axis=0)
+
+        def x_next(v):
+            return pltpu.roll(v, height - 1, 0)
+
+        def x_prev(v):
+            return pltpu.roll(v, 1, 0)
+
         @pl.loop(first, last + 1)
         def _(z):
             sh_e = lax.rem(124 - 8 * (z - 1) + 128, 128)
             sh_h = lax.rem(126 - 8 * (z - 1) + 128, 128)
-            dt = dtf[...]
-            e = [src[k, z] for k in range(3)]
-            h = [src[k, z] for k in range(3, 6)]
+            dt = take(dtf)
+            e = [take(src, k, z) for k in range(3)]
+            h = [take(src, k, z) for k in range(3, 6)]
 
             def yn(v, i):
-                edge = pltpu.roll(ye[step, i], sh_e, 1)
-                return jnp.where(lane40 == LANES - 1, edge, pltpu.roll(v, LANES - 1, 1))
+                edge = pltpu.roll(take(ye, step, i), sh_e, 1)
+                return jnp.where(lanes == LANES - 1, edge, pltpu.roll(v, LANES - 1, 1))
 
             def zn(v, i):
-                return src[i, z + 1]
+                return take(src, i, z + 1)
 
             def yp(v, i):
-                edge = pltpu.roll(yh[step, i], sh_h, 1)
-                return jnp.where(lane40 == 0, edge, pltpu.roll(v, 1, 1))
+                edge = pltpu.roll(take(yh, step, i), sh_h, 1)
+                return jnp.where(lanes == 0, edge, pltpu.roll(v, 1, 1))
 
             def zp(v, i):
-                return dst[3 + i, z - 1]
+                return take(dst, 3 + i, z - 1)
 
             h = half_h(e, h, dt, (x_next, yn, zn))
             on = jnp.where(z == ZS + 1, 1.0, 0.0)
-            e = half_e(e, h, fld[6, z], cur[...] * on, (x_prev, yp, zp))
-            for k in range(3):
-                dst[k, z] = e[k]
-                dst[3 + k, z] = h[k]
+            e = half_e(e, h, take(fld, 6, z), take(cur) * on, (x_prev, yp, zp))
+            for k in range(6):
+                v = (tuple(e) + tuple(h))[k]
+                at = 0
+                for r, n in rows:
+                    piece = v[at : at + n]
+                    at += n
+                    if keep is not None and r in keep:
+                        other, first_row, count = keep[r]
+                        ri = iota((n, LANES), 0)
+                        mine = (ri >= first_row) & (ri < first_row + count)
+                        old = other[k, z, pl.ds(r, n), :]
+                        piece = jnp.where(mine, piece, old)
+                    dst[k, z, pl.ds(r, n), :] = piece
 
     p4_first = halo_in(0, x_first)
     for c in p_copies:
@@ -443,9 +462,10 @@
     src_s[1, pl.ds(CX, 8), :] = jnp.where(low8, own4, tile4(in_sd[0, 1], in_sd[1, 1]) * m_yhi)
 
     strips_run()
-    sweep(0, fld, tmp, 6, 11)
-    sweep(1, tmp, tmp, 7, 10)
-    sweep(2, tmp, tmp, 8, 9)
+    plane = ((0, RX),)
+    sweep(0, fld, tmp, 6, 11, plane)
+    sweep(1, tmp, tmp, 7, 10, plane)
+    sweep(2, tmp, tmp, 8, 9, plane)
     own_x = pl.ds(0, CX)
     mine = pl.ds(ring * CX, CX)
     tiles[0, mine, :] = -tmp[4, ZS + 1, own_x, :]
@@ -464,8 +484,22 @@
     for c in range(4):
         for d in (4, 3, 5, 2, 6, 1, 7):
             t_copy(d, c, ring).start()
-
-    p4_second = halo_in(1, x_early + x_second)
+    for c in x_second:
+        c.start()
+
+    inner_rows = ((0, CX),)
+    sweep(0, fld, tmp, 1, NZ, inner_rows)
+    sweep(1, tmp, tmp, 1, NZ, inner_rows)
+    sweep(2, tmp, tmp, 1, NZ, inner_rows)
+
+    def store_rows(src, r, n, i):
+        return pltpu.make_async_copy(
+            src.at[pl.ds(0, 6), pl.ds(1, NZ), pl.ds(r, n), :],
+            newf_ref.at[:, :, pl.ds(r, n), :], load_sem.at[i],
+        )
+
+    stores = [store_rows(tmp, 8, 16, 2)]
+    stores[0].start()
 
     z_copies = []
     for c in range(4):
@@ -478,16 +512,18 @@
         copy.start()
         z_copies.append(copy)
 
+    p4_second = halo_in(1, x_early + x_second)
     for c in p4_second:
         c.wait_recv()
     build_strips(1)
     strips_run()
-    for step in range(3):
-        sweep(step, fld, fld, 1, NZ)
-    store = pltpu.make_async_copy(
-        fld.at[pl.ds(0, 6), pl.ds(1, NZ), pl.ds(0, CX), :], newf_ref, load_sem.at[2]
-    )
-    store.start()
+    outer_rows = ((24, 16), (0, 8))
+    sweep(0, fld, fld, 1, NZ, outer_rows)
+    sweep(1, fld, fld, 1, NZ, outer_rows)
+    sweep(2, fld, fld, 1, NZ, outer_rows, {24: (tmp, 4, 12), 0: (tmp, 0, 4)})
+    stores += [store_rows(fld, 0, 8, 3), store_rows(fld, 24, 8, 4)]
+    for c in stores[1:]:
+        c.start()
 
     for c in range(4):
         z_copies[c].wait_recv()
@@ -502,7 +538,8 @@
     for c in range(4):
         for d in range(1, 8):
             t_copy(d, c, ring).wait_send()
-    store.wait()
+    for c in stores:
+        c.wait()
 
 
 def on_device(fields, permittivity, adj_values, adj_owner, adj_row, angle_wave):
@@ -532,14 +569,8 @@
             vmem(3, 2, RX, LANES),
             vmem(RX, LANES),
             vmem(2, RX, LANES),
-            vmem(NLO, NZ, LANES),
-            vmem(NHI, NZ, LANES),
-            vmem(NLO, NZ, LANES),
-            vmem(NHI, NZ, LANES),
-            vmem(TLO, LANES),
-            vmem(THI, LANES),
-            vmem(TLO, LANES),
-            vmem(THI, LANES),
+            *[vmem(n, LANES) for _, n in PARTS_LO + PARTS_HI],
+            *[vmem(n, LANES) for _, n in PARTS_LO + PARTS_HI],
             vmem(NYS, 8, LANES),
             vmem(NYS, 8, LANES),
             vmem(RX, LANES),
@@ -552,7 +583,7 @@
             vmem(32, 8 * CX),
             vmem(4, 32, LANES),
             vmem(4, 16, LANES),
-            dma((3,)),
+            dma((5,)),
             dma((NYS,)),
             dma((NYS,)),
             dma((3, 2)),

time: 89.2 us -> 82.4 us (0.924)
  Pallas kernels: 84.9 us -> 78.2 us
    pallas_call x1, Pallas kernels: 84.9 us -> 78.2 us  [on_device(): pl.pallas_call(kernel, out_shape=(jax.ShapeDtypeStruct(fields.shape, f32)...]
where the time goes in v2:
time: 82.4 us; the launch traced here: 82.2 us
  Pallas kernels  78.2 us (95%)
  local copies, waits for them, and re-layouts  3.38 us (4%)
    pallas_call x1, Pallas kernels, on_device(): pl.pallas_call(kernel, out_shape=(jax.ShapeDtypeStruct(fields.shape, f32)...  78.2 us
    unnamed x4, local copies, waits for them, and re-layouts  3.38 us

profile of v2, /device:TPU:8, one launch (start us, length us, event | category | flops | bytes accessed | tf_op | source)
XLA Modules:
  0.0 82.2 jit_solution(8255819331407191000)
XLA Ops:
  0.6 78.2 %fdtd_far_field.1 = (f32[6,16,32,128]{3,2,1,0:T(8,128)}, f32[64,128]{1,0:T(8,128)}) custom-call(f32[6,16,32,128]{3,2,1,0:T(8,128)} %fields_ref.1, f32[16,32,128]{2,1,0:T(8,128)} %perm_ref.1, f32[96,128]{1,0:T(8,128)} %adj_ref.1, s32[1,96]{1,0:T(1,128)} %bitcast.5, s32[1,96]{1,0:T(1,128)} %bitcast.6, s32[1,128]{1,0:T(1,128)} %bitcast.7), custom_call_target="tpu_custom_call" | custom-call | tf_op jit(solution)/shard_map/fdtd_far_field/pallas_call | solution.py:552
  78.8 0.0 copy-start
  78.8 2.8 %copy.10 = f32[6,16,32,128]{3,2,1,0:T(8,128)} copy(f32[6,16,32,128]{3,2,1,0:T(8,128)} %get-tuple-element.8) | data formatting | bytes 3145728
  81.6 0.0 copy-done
  81.6 0.6 copy.11
Async XLA Ops:
  78.8 2.8 %copy-start = (f32[64,128]{1,0:T(8,128)S(1)}, f32[64,128]{1,0:T(8,128)}, u32[]{:S(2)}) copy-start(f32[64,128]{1,0:T(8,128)} %get-tuple-element.5) | copy-start | bytes 98308

commit v3 on v2

--- a/solution.py
+++ b/solution.py
@@ -484,8 +484,8 @@
     for c in range(4):
         for d in (4, 3, 5, 2, 6, 1, 7):
             t_copy(d, c, ring).start()
-    for c in x_second:
-        c.start()
+        if c >= 2:
+            x_second[c - 2].start()
 
     inner_rows = ((0, CX),)
     sweep(0, fld, tmp, 1, NZ, inner_rows)

time: 82.4 us -> 82.4 us (level)
  no operation moved by 1% of the time
where the time goes in v3:
time: 82.4 us; the launch traced here: 82.2 us
  Pallas kernels  78.2 us (95%)
  local copies, waits for them, and re-layouts  3.38 us (4%)
    pallas_call x1, Pallas kernels, on_device(): pl.pallas_call(kernel, out_shape=(jax.ShapeDtypeStruct(fields.shape, f32)...  78.2 us
    unnamed x4, local copies, waits for them, and re-layouts  3.38 us

profile of v3, /device:TPU:8, one launch (start us, length us, event | category | flops | bytes accessed | tf_op | source)
XLA Modules:
  0.0 82.2 jit_solution(9218420813413559820)
XLA Ops:
  0.6 78.2 %fdtd_far_field.1 = (f32[6,16,32,128]{3,2,1,0:T(8,128)}, f32[64,128]{1,0:T(8,128)}) custom-call(f32[6,16,32,128]{3,2,1,0:T(8,128)} %fields_ref.1, f32[16,32,128]{2,1,0:T(8,128)} %perm_ref.1, f32[96,128]{1,0:T(8,128)} %adj_ref.1, s32[1,96]{1,0:T(1,128)} %bitcast.5, s32[1,96]{1,0:T(1,128)} %bitcast.6, s32[1,128]{1,0:T(1,128)} %bitcast.7), custom_call_target="tpu_custom_call" | custom-call | tf_op jit(solution)/shard_map/fdtd_far_field/pallas_call | solution.py:552
  78.8 0.0 copy-start
  78.8 2.8 %copy.10 = f32[6,16,32,128]{3,2,1,0:T(8,128)} copy(f32[6,16,32,128]{3,2,1,0:T(8,128)} %get-tuple-element.8) | data formatting | bytes 3145728
  81.6 0.0 copy-done
  81.6 0.6 copy.11
Async XLA Ops:
  78.8 2.8 %copy-start = (f32[64,128]{1,0:T(8,128)S(1)}, f32[64,128]{1,0:T(8,128)}, u32[]{:S(2)}) copy-start(f32[64,128]{1,0:T(8,128)} %get-tuple-element.5) | copy-start | bytes 98308
